TPU v7x, 256 devices: a whole 4x4x8 slice. The times are simulated.
256 devices in a mesh: slot: 8 (over y, core), asset: 32 (over x, z).
Axes of the slice: x: 4, y: 4, z: 8, core: 2. Of those that a mesh axis runs over, the one named last changes fastest.
Arguments:
- slot_emb: bfloat16 [16384, 768], P(('slot', 'asset')), may hold values from -4 to 4
- asset_panel: bfloat16 [768, 32768], P('slot', 'asset'), may hold values from -4 to 4
- mult: int32 [16384], P('slot'), may hold values from 1 to 4
- caps: int32 [32768], P('asset'), may hold values from 1 to 8, as said below
Outputs:
- plan: float32 [16384, 32768], P('slot', 'asset')
Inputs may be any that keep to these rules, and one draw needn't show every extreme that they name: caps are whole numbers; the last asset's cap is the largest.
All inputs are finite; a program needn't handle non-finite values.
Results may differ from a plain program's by a relative error of at most 0.0003.
Values may be sent and summed in bfloat16 or wider, within the bound.
No kernel may reach another device: no remote copies, remote signals or barrier semaphores. Data moves between devices by JAX's collectives and lax.ppermute only.
A program may use at most 64 MiB of HBM per device.

v0:
```python
import jax
import jax.numpy as jnp
from jax import lax
from jax.sharding import PartitionSpec as P

EMB = 768
ITERS = 3


def row_side(logits, asset_pot):
    shifted = logits + asset_pot[None, :]
    peak = lax.pmax(jnp.max(shifted, axis=1), "asset")
    total = lax.psum(jnp.sum(jnp.exp(shifted - peak[:, None]), axis=1), "asset")
    return peak + jnp.log(total)


def col_side(logits, slot_pot):
    shifted = logits + slot_pot[:, None]
    peak = lax.pmax(jnp.max(shifted, axis=0), "slot")
    total = lax.psum(jnp.sum(jnp.exp(shifted - peak[None, :]), axis=0), "slot")
    return peak + jnp.log(total)


def per_device(slot_emb, asset_panel, mult, caps):
    slot_block = lax.all_gather(slot_emb, "asset", axis=0, tiled=True)
    logits = jnp.dot(
        slot_block,
        lax.all_gather(asset_panel, "slot", axis=0, tiled=True),
        preferred_element_type=jnp.float32,
    ) * EMB ** (-0.5)
    caps_float = caps.astype(jnp.float32)
    cap_total = lax.psum(jnp.sum(caps_float), "asset")
    log_b = jnp.log(caps_float) - jnp.log(cap_total)
    log_a = jnp.log(mult.astype(jnp.float32))
    asset_pot = jnp.zeros((logits.shape[1],), jnp.float32)
    slot_pot = jnp.zeros((logits.shape[0],), jnp.float32)
    for iteration in range(ITERS):
        slot_pot = log_a - row_side(logits, asset_pot)
        asset_pot = log_b - col_side(logits, slot_pot)
    factor = float(
        logits.shape[0] * lax.axis_size("slot") * logits.shape[1] * lax.axis_size("asset")
    )
    return jnp.exp(logits + slot_pot[:, None] + asset_pot[None, :]) * factor


def solution(mesh):
    return jax.shard_map(
        per_device,
        mesh=mesh,
        in_specs=(P(("slot", "asset"), None), P("slot", "asset"), P("slot"), P("asset")),
        out_specs=P("slot", "asset"),
        check_vma=False,
    )
```

profile of v0, /device:TPU:1, one launch (start us, length us, event | category | flops | bytes accessed | tf_op | source)
XLA Modules:
  0.0 697.3 jit_solution(16595806168147780768)
XLA Ops:
  6.5 0.0 all-gather.5.cloned.1.call-start
  6.5 0.7 all-gather.5.cloned.1.call-update
  7.3 0.0 all-gather.3.cloned.1.call-start
  7.3 0.7 all-gather.3.cloned.1.call-update
  8.0 1.3 convert_reduce_fusion
  9.3 31.0 %all-gather.5.cloned.1.call-done = bf16[768,1024]{1,0:T(8,128)(2,1)} async-done(((bf16[96,1024]{1,0:T(8,128)(2,1)}), bf16[768,1024]{1,0:T(8,128)(2,1)}) %all-gather.5.cloned.1.call-update) | async-done | bytes 1572880 | tf_op jit(solution)/shard_map/all_gather | solution.py:28
  40.3 77.9 %all-gather.3.cloned.1.call-done = bf16[2048,768]{1,0:T(8,128)(2,1)} async-done(((bf16[64,768]{1,0:T(8,128)(2,1)}), bf16[2048,768]{1,0:T(8,128)(2,1)}) %all-gather.3.cloned.1.call-update) | async-done | bytes 3145744 | tf_op jit(solution)/shard_map/all_gather | solution.py:25
  118.2 9.2 %fusion = (f32[2048]{0:T(1024)S(1)}, f32[2048,1024]{1,0:T(8,128)}) fusion(bf16[2048,768]{1,0:T(8,128)(2,1)} %all-gather.3.cloned.1.call-done, bf16[768,1024]{1,0:T(8,128)(2,1)} %all-gather.5.cloned.1.call-done), kind=kOutput, calls=%fused_computation.22 | convolution fusion | flops 3225417728 | bytes 13115392 | tf_op jit(solution)/shard_map/dot_general | solution.py:26
  127.4 0.0 copy-start
  127.4 58.9 %pmax.42 = f32[2048]{0:T(1024)S(1)} all-reduce(f32[2048]{0:T(1024)S(1)} %get-tuple-element.7), channel_id=1, replica_groups=mesh['slot'=8,'asset'=32] {'asset'}, use_global_device_ids=true, to_apply=%region_3.0 | all-reduce | flops 2048 | bytes 16384 | tf_op jit(solution)/shard_map/pmax | solution.py:12
  186.3 4.4 exponential_reduce_fusion.5
  190.7 58.3 %all-reduce = (f32[2048]{0:T(1024)S(1)}, f32[]{:T(128)}) all-reduce(f32[2048]{0:T(1024)S(1)} %exponential_reduce_fusion.5, f32[]{:T(128)} %convert_reduce_fusion), channel_id=1, replica_groups=mesh['slot'=8,'asset'=32] {'asset'}, use_global_device_ids=true, to_apply=%region_5.0 | all-reduce | flops 2049 | bytes 16392 | tf_op jit(solution)/shard_map/psum | solution.py:13
  249.6 0.0 copy-done
  249.6 0.0 copy-start.1
  249.6 4.0 add_reduce_fusion.3
  253.6 44.0 %pmax.43 = f32[1024]{0:T(1024)S(1)} all-reduce(f32[1024]{0:T(1024)S(1)} %add_reduce_fusion.3), channel_id=1, replica_groups=mesh['slot'=8,'asset'=32] {'slot'}, use_global_device_ids=true, to_apply=%region_7.0 | all-reduce | flops 1024 | bytes 8192 | tf_op jit(solution)/shard_map/pmax | solution.py:19
  297.6 4.2 exponential_reduce_fusion.4
  301.9 12.4 %psum.51 = f32[1024]{0:T(1024)S(1)} all-reduce(f32[1024]{0:T(1024)S(1)} %exponential_reduce_fusion.4), channel_id=1, replica_groups=mesh['slot'=8,'asset'=32] {'slot'}, use_global_device_ids=true, to_apply=%region_9.0 | all-reduce | flops 1024 | bytes 8192 | tf_op jit(solution)/shard_map/psum | solution.py:20
  314.3 0.0 copy-done.1
  314.3 4.0 add_reduce_fusion.2
  318.3 59.1 %pmax.44 = f32[2048]{0:T(1024)S(1)} all-reduce(f32[2048]{0:T(1024)S(1)} %add_reduce_fusion.2), channel_id=1, replica_groups=mesh['slot'=8,'asset'=32] {'asset'}, use_global_device_ids=true, to_apply=%region_11.0 | all-reduce | flops 2048 | bytes 16384 | tf_op jit(solution)/shard_map/pmax | solution.py:12
  377.5 4.4 exponential_reduce_fusion.3
  381.8 57.1 %psum.52 = f32[2048]{0:T(1024)S(1)} all-reduce(f32[2048]{0:T(1024)S(1)} %exponential_reduce_fusion.3), channel_id=1, replica_groups=mesh['slot'=8,'asset'=32] {'asset'}, use_global_device_ids=true, to_apply=%region_13.0 | all-reduce | flops 2048 | bytes 16384 | tf_op jit(solution)/shard_map/psum | solution.py:13
  438.9 4.0 add_reduce_fusion.1
  442.9 39.6 %pmax.45 = f32[1024]{0:T(1024)S(1)} all-reduce(f32[1024]{0:T(1024)S(1)} %add_reduce_fusion.1), channel_id=1, replica_groups=mesh['slot'=8,'asset'=32] {'slot'}, use_global_device_ids=true, to_apply=%region_15.0 | all-reduce | flops 1024 | bytes 8192 | tf_op jit(solution)/shard_map/pmax | solution.py:19
  482.5 4.2 exponential_reduce_fusion.2
  486.8 12.4 %psum.53 = f32[1024]{0:T(1024)S(1)} all-reduce(f32[1024]{0:T(1024)S(1)} %exponential_reduce_fusion.2), channel_id=1, replica_groups=mesh['slot'=8,'asset'=32] {'slot'}, use_global_device_ids=true, to_apply=%region_17.0 | all-reduce | flops 1024 | bytes 8192 | tf_op jit(solution)/shard_map/psum | solution.py:20
  499.2 4.0 add_reduce_fusion
  503.2 59.2 %pmax.46 = f32[2048]{0:T(1024)S(1)} all-reduce(f32[2048]{0:T(1024)S(1)} %add_reduce_fusion), channel_id=1, replica_groups=mesh['slot'=8,'asset'=32] {'asset'}, use_global_device_ids=true, to_apply=%region_19.0 | all-reduce | flops 2048 | bytes 16384 | tf_op jit(solution)/shard_map/pmax | solution.py:12
  562.4 4.4 exponential_reduce_fusion.1
  566.7 57.0 %psum.54 = f32[2048]{0:T(1024)S(1)} all-reduce(f32[2048]{0:T(1024)S(1)} %exponential_reduce_fusion.1), channel_id=1, replica_groups=mesh['slot'=8,'asset'=32] {'asset'}, use_global_device_ids=true, to_apply=%region_21.0 | all-reduce | flops 2048 | bytes 16384 | tf_op jit(solution)/shard_map/psum | solution.py:13
  623.8 4.0 add_reduce_fusion.4
  627.8 39.6 %pmax.47 = f32[1024]{0:T(1024)S(1)} all-reduce(f32[1024]{0:T(1024)S(1)} %add_reduce_fusion.4), channel_id=1, replica_groups=mesh['slot'=8,'asset'=32] {'slot'}, use_global_device_ids=true, to_apply=%region_23.0 | all-reduce | flops 1024 | bytes 8192 | tf_op jit(solution)/shard_map/pmax | solution.py:19
  667.4 4.2 exponential_reduce_fusion
  671.7 12.4 %psum.55 = f32[1024]{0:T(1024)S(1)} all-reduce(f32[1024]{0:T(1024)S(1)} %exponential_reduce_fusion), channel_id=1, replica_groups=mesh['slot'=8,'asset'=32] {'slot'}, use_global_device_ids=true, to_apply=%region_25.0 | all-reduce | flops 1024 | bytes 8192 | tf_op jit(solution)/shard_map/psum | solution.py:20
  684.1 6.3 exponential_multiply_fusion
  (6 shorter events, 0.1 us)
Async XLA Ops:
  6.5 33.7 %all-gather.5.cloned.1.call-start = ((), (), s32[]{:S(2)}) async-start(), calls=%async_computation.1 | async-start | bytes 1769472 | tf_op jit(solution)/shard_map/all_gather | solution.py:28
  7.3 110.9 %all-gather.3.cloned.1.call-start = ((), (), s32[]{:S(2)}) async-start(), calls=%async_computation | async-start | bytes 3244032 | tf_op jit(solution)/shard_map/all_gather | solution.py:25
  127.4 122.2 %copy-start = (s32[2048]{0:T(1024)S(1)}, s32[2048]{0:T(1024)}, u32[]{:S(2)}) copy-start(s32[2048]{0:T(1024)} %param.6) | copy-start | bytes 24580
  249.6 64.7 %copy-start.1 = (s32[1024]{0:T(1024)S(1)}, s32[1024]{0:T(1024)}, u32[]{:S(2)}) copy-start(s32[1024]{0:T(1024)} %param.7) | copy-start | bytes 12292
Sparse Core Ops, SparseCore 0:
  9.2 31.0 all-gather.4
  42.8 75.2 all-gather.2
where the time goes:
time: 698 us; the launch traced here: 697 us
  blocking collectives  510 us (73%)
  waiting for transfers between devices  110 us (16%)
  other arithmetic  53.5 us (8%)
  between operations  14.2 us (2%)
  matrix products  9.19 us (1%)
    pmax x3, blocking collectives, row_side(): peak = lax.pmax(jnp.max(shifted, axis=1), 'asset')  177 us
    psum x3, blocking collectives, row_side(): total = lax.psum(jnp.sum(jnp.exp(shifted - peak[:, None]), axis=1), 'asset')  172 us
    pmax x3, blocking collectives, col_side(): peak = lax.pmax(jnp.max(shifted, axis=0), 'slot')  123 us
    all_gather x1, waiting for transfers between devices, per_device(): slot_block = lax.all_gather(slot_emb, 'asset', axis=0, tiled=True)  77.9 us
    psum x3, blocking collectives, col_side(): total = lax.psum(jnp.sum(jnp.exp(shifted - peak[None, :]), axis=0), 'slot')  37.3 us
    all_gather x1, waiting for transfers between devices, per_device(): lax.all_gather(asset_panel, 'slot', axis=0, tiled=True)  31 us
  transfers between devices with their start and end apart: 2, of which 2 were waited for; matrix products, arithmetic and copies ran while one was open for 0% of the time, Pallas kernels for 0%

commit v1 on v0

--- a/solution.py
+++ b/solution.py
@@ -22,7 +22,9 @@
 
 
 def per_device(slot_emb, asset_panel, mult, caps):
-    slot_block = lax.all_gather(slot_emb, "asset", axis=0, tiled=True)
+    slot_block = jnp.concatenate(
+        lax.all_to_all(jnp.stack([slot_emb] * lax.axis_size("asset")), "asset", 0, 0), axis=0
+    )
     logits = jnp.dot(
         slot_block,
         lax.all_gather(asset_panel, "slot", axis=0, tiled=True),

time: 698 us -> 670 us (0.960)
  waiting for transfers between devices: 110 us -> 70.9 us
  starting transfers between devices: 0.04 us -> 11.9 us
    all_gather x1 -> x0, waiting for transfers between devices: 77.9 us -> none  [per_device(): slot_block = lax.all_gather(slot_emb, 'asset', axis=0, tiled=True)]
    all_to_all x0 -> x1, waiting for transfers between devices: none -> 39.8 us  [per_device(): lax.all_to_all(jnp.stack([slot_emb] * lax.axis_size('asset')), 'asset', 0...]
    all_to_all x0 -> x1, starting transfers between devices: none -> 11.9 us  [per_device(): lax.all_to_all(jnp.stack([slot_emb] * lax.axis_size('asset')), 'asset', 0...]
where the time goes in v1:
time: 670 us
  blocking collectives  510 us (76%)
  waiting for transfers between devices  70.9 us (11%)
  other arithmetic  52.9 us (8%)
  between operations  14.2 us (2%)
  starting transfers between devices  11.9 us (2%)
  matrix products  7.11 us (1%)
    pmax x3, blocking collectives, row_side(): peak = lax.pmax(jnp.max(shifted, axis=1), 'asset')  177 us
    psum x3, blocking collectives, row_side(): total = lax.psum(jnp.sum(jnp.exp(shifted - peak[:, None]), axis=1), 'asset')  174 us
    pmax x3, blocking collectives, col_side(): peak = lax.pmax(jnp.max(shifted, axis=0), 'slot')  122 us
    all_to_all x1, waiting for transfers between devices, per_device(): lax.all_to_all(jnp.stack([slot_emb] * lax.axis_size('asset')), 'asset', 0...  39.8 us
    psum x3, blocking collectives, col_side(): total = lax.psum(jnp.sum(jnp.exp(shifted - peak[None, :]), axis=0), 'slot')  37.1 us
    all_gather x1, waiting for transfers between devices, per_device(): lax.all_gather(asset_panel, 'slot', axis=0, tiled=True)  30.3 us
  transfers between devices with their start and end apart: 2, of which 2 were waited for; matrix products, arithmetic and copies ran while one was open for 0% of the time, Pallas kernels for 0%

profile of v1, /device:TPU:1, one launch (start us, length us, event | category | flops | bytes accessed | tf_op | source)
XLA Modules:
  0.0 669.5 jit_solution(4915027837957662886)
XLA Ops:
  6.5 0.0 copy-start.1
  6.5 2.9 stack.2
  9.5 11.9 %all-to-all-start = ((bf16[32,64,768]{2,1,0:T(8,128)(2,1)}), bf16[32,64,768]{2,1,0:T(8,128)(2,1)S(1)}, u32[]{:S(2)}, u32[]{:S(2)}) async-start(bf16[32,64,768]{2,1,0:T(8,128)(2,1)} %stack.2), calls=%async_computation | async-start | bytes 6291456 | tf_op jit(solution)/shard_map/all_to_all | solution.py:26
  21.3 0.0 all-gather.2.cloned.1.call-start
  21.4 0.7 all-gather.2.cloned.1.call-update
  22.1 0.0 copy-done.1
  22.1 0.6 convert_reduce_fusion
  22.7 30.3 %all-gather.2.cloned.1.call-done = bf16[768,1024]{1,0:T(8,128)(2,1)} async-done(((bf16[96,1024]{1,0:T(8,128)(2,1)}), bf16[768,1024]{1,0:T(8,128)(2,1)}) %all-gather.2.cloned.1.call-update) | async-done | bytes 1572880 | tf_op jit(solution)/shard_map/all_gather | solution.py:30
  53.1 39.8 %all-to-all-done = bf16[32,64,768]{2,1,0:T(8,128)(2,1)S(1)} async-done(((bf16[32,64,768]{2,1,0:T(8,128)(2,1)}), bf16[32,64,768]{2,1,0:T(8,128)(2,1)S(1)}, u32[]{:S(2)}, u32[]{:S(2)}) %all-to-all-start) | async-done | bytes 3145760 | tf_op jit(solution)/shard_map/all_to_all | solution.py:26
  92.9 7.1 %fusion = (f32[2048]{0:T(1024)S(1)}, f32[2048,1024]{1,0:T(8,128)}) fusion(bf16[2048,768]{1,0:T(8,128)(2,1)S(1)} %bitcast.3, bf16[768,1024]{1,0:T(8,128)(2,1)} %all-gather.2.cloned.1.call-done), kind=kOutput, calls=%fused_computation.22 | convolution fusion | flops 3225417728 | bytes 13115392 | tf_op jit(solution)/shard_map/dot_general | solution.py:28
  100.0 0.0 copy-start
  100.0 60.6 %pmax.42 = f32[2048]{0:T(1024)S(1)} all-reduce(f32[2048]{0:T(1024)S(1)} %get-tuple-element.7), channel_id=1, replica_groups=mesh['slot'=8,'asset'=32] {'asset'}, use_global_device_ids=true, to_apply=%region_3.0 | all-reduce | flops 2048 | bytes 16384 | tf_op jit(solution)/shard_map/pmax | solution.py:12
  160.6 4.4 exponential_reduce_fusion.5
  165.0 58.8 %all-reduce = (f32[2048]{0:T(1024)S(1)}, f32[]{:T(128)}) all-reduce(f32[2048]{0:T(1024)S(1)} %exponential_reduce_fusion.5, f32[]{:T(128)} %convert_reduce_fusion), channel_id=1, replica_groups=mesh['slot'=8,'asset'=32] {'asset'}, use_global_device_ids=true, to_apply=%region_5.0 | all-reduce | flops 2049 | bytes 16392 | tf_op jit(solution)/shard_map/psum | solution.py:13
  224.5 0.0 copy-done
  224.5 4.0 add_reduce_fusion.3
  228.5 41.5 %pmax.43 = f32[1024]{0:T(1024)S(1)} all-reduce(f32[1024]{0:T(1024)S(1)} %add_reduce_fusion.3), channel_id=1, replica_groups=mesh['slot'=8,'asset'=32] {'slot'}, use_global_device_ids=true, to_apply=%region_7.0 | all-reduce | flops 1024 | bytes 8192 | tf_op jit(solution)/shard_map/pmax | solution.py:19
  270.0 4.2 exponential_reduce_fusion.4
  274.2 12.3 %psum.51 = f32[1024]{0:T(1024)S(1)} all-reduce(f32[1024]{0:T(1024)S(1)} %exponential_reduce_fusion.4), channel_id=1, replica_groups=mesh['slot'=8,'asset'=32] {'slot'}, use_global_device_ids=true, to_apply=%region_9.0 | all-reduce | flops 1024 | bytes 8192 | tf_op jit(solution)/shard_map/psum | solution.py:20
  286.5 4.0 add_reduce_fusion.2
  290.5 58.1 %pmax.44 = f32[2048]{0:T(1024)S(1)} all-reduce(f32[2048]{0:T(1024)S(1)} %add_reduce_fusion.2), channel_id=1, replica_groups=mesh['slot'=8,'asset'=32] {'asset'}, use_global_device_ids=true, to_apply=%region_11.0 | all-reduce | flops 2048 | bytes 16384 | tf_op jit(solution)/shard_map/pmax | solution.py:12
  348.7 4.4 exponential_reduce_fusion.3
  353.1 57.6 %psum.52 = f32[2048]{0:T(1024)S(1)} all-reduce(f32[2048]{0:T(1024)S(1)} %exponential_reduce_fusion.3), channel_id=1, replica_groups=mesh['slot'=8,'asset'=32] {'asset'}, use_global_device_ids=true, to_apply=%region_13.0 | all-reduce | flops 2048 | bytes 16384 | tf_op jit(solution)/shard_map/psum | solution.py:13
  410.6 4.0 add_reduce_fusion.1
  414.7 40.1 %pmax.45 = f32[1024]{0:T(1024)S(1)} all-reduce(f32[1024]{0:T(1024)S(1)} %add_reduce_fusion.1), channel_id=1, replica_groups=mesh['slot'=8,'asset'=32] {'slot'}, use_global_device_ids=true, to_apply=%region_15.0 | all-reduce | flops 1024 | bytes 8192 | tf_op jit(solution)/shard_map/pmax | solution.py:19
  454.8 4.2 exponential_reduce_fusion.2
  459.0 12.4 %psum.53 = f32[1024]{0:T(1024)S(1)} all-reduce(f32[1024]{0:T(1024)S(1)} %exponential_reduce_fusion.2), channel_id=1, replica_groups=mesh['slot'=8,'asset'=32] {'slot'}, use_global_device_ids=true, to_apply=%region_17.0 | all-reduce | flops 1024 | bytes 8192 | tf_op jit(solution)/shard_map/psum | solution.py:20
  471.4 4.0 add_reduce_fusion
  475.5 58.1 %pmax.46 = f32[2048]{0:T(1024)S(1)} all-reduce(f32[2048]{0:T(1024)S(1)} %add_reduce_fusion), channel_id=1, replica_groups=mesh['slot'=8,'asset'=32] {'asset'}, use_global_device_ids=true, to_apply=%region_19.0 | all-reduce | flops 2048 | bytes 16384 | tf_op jit(solution)/shard_map/pmax | solution.py:12
  533.6 4.4 exponential_reduce_fusion.1
  537.9 57.6 %psum.54 = f32[2048]{0:T(1024)S(1)} all-reduce(f32[2048]{0:T(1024)S(1)} %exponential_reduce_fusion.1), channel_id=1, replica_groups=mesh['slot'=8,'asset'=32] {'asset'}, use_global_device_ids=true, to_apply=%region_21.0 | all-reduce | flops 2048 | bytes 16384 | tf_op jit(solution)/shard_map/psum | solution.py:13
  595.6 4.0 add_reduce_fusion.4
  599.6 40.1 %pmax.47 = f32[1024]{0:T(1024)S(1)} all-reduce(f32[1024]{0:T(1024)S(1)} %add_reduce_fusion.4), channel_id=1, replica_groups=mesh['slot'=8,'asset'=32] {'slot'}, use_global_device_ids=true, to_apply=%region_23.0 | all-reduce | flops 1024 | bytes 8192 | tf_op jit(solution)/shard_map/pmax | solution.py:19
  639.7 4.2 exponential_reduce_fusion
  643.9 12.4 %psum.55 = f32[1024]{0:T(1024)S(1)} all-reduce(f32[1024]{0:T(1024)S(1)} %exponential_reduce_fusion), channel_id=1, replica_groups=mesh['slot'=8,'asset'=32] {'slot'}, use_global_device_ids=true, to_apply=%region_25.0 | all-reduce | flops 1024 | bytes 8192 | tf_op jit(solution)/shard_map/psum | solution.py:20
  656.3 6.4 exponential_multiply_fusion
  (6 shorter events, 0.1 us)
Async XLA Ops:
  6.5 15.5 %copy-start.1 = (s32[1024]{0:T(1024)S(1)}, s32[1024]{0:T(1024)}, u32[]{:S(2)}) copy-start(s32[1024]{0:T(1024)} %param.7) | copy-start | bytes 12292
  9.5 83.4 %all-to-all-start = ((bf16[32,64,768]{2,1,0:T(8,128)(2,1)}), bf16[32,64,768]{2,1,0:T(8,128)(2,1)S(1)}, u32[]{:S(2)}, u32[]{:S(2)}) async-start(bf16[32,64,768]{2,1,0:T(8,128)(2,1)} %stack.2), calls=%async_computation | async-start | bytes 6291456 | tf_op jit(solution)/shard_map/all_to_all | solution.py:26
  21.3 31.7 %all-gather.2.cloned.1.call-start = ((), (), s32[]{:S(2)}) async-start(), calls=%async_computation.1 | async-start | bytes 1769472 | tf_op jit(solution)/shard_map/all_gather | solution.py:30
  100.0 124.5 %copy-start = (s32[2048]{0:T(1024)S(1)}, s32[2048]{0:T(1024)}, u32[]{:S(2)}) copy-start(s32[2048]{0:T(1024)} %param.6) | copy-start | bytes 24580
Sparse Core Ops, SparseCore 0:
  24.0 29.0 all-gather.1
